TPU v7x, 256 devices: a whole 4x4x8 slice. The times are simulated.
256 devices in a mesh: ia: 4 (over y), ja: 4 (over x), ka: 16 (over z, core).
Axes of the slice: x: 4, y: 4, z: 8, core: 2. Of those that a mesh axis runs over, the one named last changes fastest.
Arguments:
- blocks: bfloat16 [4, 4, 16, 2, 128, 128, 128], P('ia', 'ja', 'ka'), may hold values from -6 to 6
- first_mode_rows: int32 [4, 4, 16, 2], P('ia', 'ja', 'ka'), may hold values from 0 to 15
- second_mode_rows: int32 [4, 4, 16, 2], P('ia', 'ja', 'ka'), may hold values from 0 to 15
- third_mode_rows: int32 [4, 4, 16, 2], P('ia', 'ja', 'ka'), may hold values from 0 to 3
- filled: int32 [4, 4, 16], P('ia', 'ja', 'ka'), may hold values from 1 to 2, as said below
- owner_one: int32 [64], replicated, may hold values from 0 to 63, each once
- owner_two: int32 [64], replicated, may hold values from 0 to 63, each once
- factor_b: float32 [4, 2048, 256], P('ja', ('ia', 'ka'))
- factor_c: float32 [16, 512, 256], P('ka')
Outputs:
- a_new: float32 [4, 2048, 256], P('ia', ('ja', 'ka'))
- b_new: float32 [4, 2048, 256], P('ja', ('ia', 'ka'))
Inputs may be any that keep to these rules, and one draw needn't show every extreme that they name: Number of nonempty slots of a grid cell; at least one cell has all 2 slots filled. Slots at or beyond this count hold data that is not part of the tensor.
All inputs are finite; a program needn't handle non-finite values.
Results may differ from a plain program's by a relative error of at most 0.0039.
The roundings to bfloat16 on the way count: a program that leaves them out, or rounds other values in their place, can miss the bound.
Values may be sent and summed in bfloat16 or wider, within the bound.
A program may use at most 128 MiB of HBM per device.

v0:
```python
import jax
import jax.numpy as jnp
from jax import lax
from jax.sharding import PartitionSpec as P

EPS = 1e-06


def solve_rows(gram, rows):
    lower = jnp.linalg.cholesky(gram)
    return jax.scipy.linalg.cho_solve((lower, True), rows.T).T


def add_rows(accum, start, contrib):
    current = lax.dynamic_slice_in_dim(accum, start, contrib.shape[0], 0)
    return lax.dynamic_update_slice_in_dim(accum, current + contrib, start, 0)


def batched_sum(inner, weights):
    summed = lax.dot_general(
        inner,
        weights.astype(jnp.float32),
        (((1,), (0,)), ((2,), (1,))),
        precision=lax.Precision.HIGHEST,
        preferred_element_type=jnp.float32,
    )
    return summed.T


def to_logical(stored, owner, piece_rows):
    return stored.reshape(-1, piece_rows, stored.shape[1])[owner].reshape(stored.shape)


def to_stored(logical, owner, piece_rows):
    positions = jnp.arange(owner.shape[0], dtype=jnp.int32)
    inverse = jnp.sum(
        jnp.where(owner[None, :] == positions[:, None], positions[None, :], 0), axis=1
    )
    return logical.reshape(-1, piece_rows, logical.shape[1])[inverse].reshape(logical.shape)


def keep_same(value):
    return value


def partial_value(function, slot):

    def applied(value):
        return function(value, slot)

    return applied


def body(
    blocks,
    first_mode_rows,
    second_mode_rows,
    third_mode_rows,
    filled,
    owner_one,
    owner_two,
    factor_b,
    factor_c,
):
    highest = lax.Precision.HIGHEST
    piece_rows = factor_b.shape[1]
    rank_width = factor_b.shape[2]
    block_edge = blocks.shape[-1]
    slot_count = blocks.shape[3]
    total_one = piece_rows * lax.axis_size("ia") * lax.axis_size("ja") * lax.axis_size("ka")
    slab_rows_one = piece_rows * lax.axis_size("ja") * lax.axis_size("ka")
    slab_rows_two = piece_rows * lax.axis_size("ia") * lax.axis_size("ka")
    own_b = factor_b[0]
    own_c = lax.dynamic_slice_in_dim(
        factor_c[0], lax.axis_index(("ia", "ja")) * piece_rows, piece_rows, 0
    )
    local_b = jnp.dot(own_b.T, own_b, precision=highest, preferred_element_type=jnp.float32)
    local_c = jnp.dot(own_c.T, own_c, precision=highest, preferred_element_type=jnp.float32)
    gram_b, gram_c = lax.psum((local_b, local_c), ("ia", "ja", "ka"))
    stored_b = lax.all_gather(factor_b.astype(jnp.bfloat16), ("ia", "ka"), axis=1, tiled=True)[0]
    half_b = to_logical(stored_b, owner_two, piece_rows)
    half_c = factor_c[0].astype(jnp.bfloat16)
    live_count = filled[0, 0, 0]

    def update_one(partial_sum, slot):
        block = blocks[0, 0, 0, slot]
        b_rows = lax.dynamic_slice_in_dim(
            half_b, second_mode_rows[0, 0, 0, slot] * block_edge, block_edge, 0
        )
        c_rows = lax.dynamic_slice_in_dim(
            half_c, third_mode_rows[0, 0, 0, slot] * block_edge, block_edge, 0
        )
        inner = jnp.dot(
            block.reshape(block_edge * block_edge, block_edge),
            c_rows,
            preferred_element_type=jnp.float32,
        )
        inner = inner.reshape(block_edge, block_edge, rank_width)
        contrib = batched_sum(inner, b_rows)
        return add_rows(partial_sum, first_mode_rows[0, 0, 0, slot] * block_edge, contrib)

    partial_one = jnp.zeros((slab_rows_one, rank_width), jnp.float32)
    for slot in range(slot_count):
        partial_one = lax.cond(
            slot < live_count, partial_value(update_one, slot), keep_same, partial_one
        )
    stored_one = to_stored(partial_one, owner_one, piece_rows)
    system_one = gram_b * gram_c
    summed_own = lax.psum_scatter(stored_one, ("ja", "ka"), scatter_dimension=0, tiled=True)
    a_hat = solve_rows(system_one, summed_own)
    squares_a = lax.psum(jnp.sum(a_hat * a_hat, axis=0), ("ia", "ja", "ka"))
    scale_a = jnp.sqrt(squares_a / total_one + EPS)
    a_own = a_hat / scale_a
    local_a = jnp.dot(a_own.T, a_own, precision=highest, preferred_element_type=jnp.float32)
    gram_a = lax.psum(local_a, ("ia", "ja", "ka"))
    stored_a = lax.all_gather(a_own.astype(jnp.bfloat16)[None], ("ja", "ka"), axis=1, tiled=True)[0]
    half_a = to_logical(stored_a, owner_one, piece_rows)

    def update_two(partial_sum, slot):
        block = blocks[0, 0, 0, slot]
        a_rows = lax.dynamic_slice_in_dim(
            half_a, first_mode_rows[0, 0, 0, slot] * block_edge, block_edge, 0
        )
        c_rows = lax.dynamic_slice_in_dim(
            half_c, third_mode_rows[0, 0, 0, slot] * block_edge, block_edge, 0
        )
        inner = lax.dot_general(
            block.reshape(block_edge, block_edge * block_edge),
            a_rows,
            (((0,), (0,)), ((), ())),
            preferred_element_type=jnp.float32,
        )
        inner = inner.reshape(block_edge, block_edge, rank_width)
        contrib = batched_sum(inner, c_rows)
        return add_rows(partial_sum, second_mode_rows[0, 0, 0, slot] * block_edge, contrib)

    partial_two = jnp.zeros((slab_rows_two, rank_width), jnp.float32)
    for slot in range(slot_count):
        partial_two = lax.cond(
            slot < live_count, partial_value(update_two, slot), keep_same, partial_two
        )
    stored_two = to_stored(partial_two, owner_two, piece_rows)
    summed_two = lax.psum_scatter(stored_two, ("ia", "ka"), scatter_dimension=0, tiled=True)
    b_hat = solve_rows(gram_a * gram_c, summed_two)
    squares_b = lax.psum(jnp.sum(b_hat * b_hat, axis=0), ("ia", "ja", "ka"))
    b_own = b_hat / jnp.sqrt(squares_b / total_one + EPS)
    return (a_own[None], b_own[None])


def solution(mesh):
    return jax.shard_map(
        body,
        mesh=mesh,
        in_specs=(
            P("ia", "ja", "ka", None, None, None, None),
            P("ia", "ja", "ka", None),
            P("ia", "ja", "ka", None),
            P("ia", "ja", "ka", None),
            P("ia", "ja", "ka"),
            P(),
            P(),
            P("ja", ("ia", "ka"), None),
            P("ka", None, None),
        ),
        out_specs=(P("ia", ("ja", "ka"), None), P("ja", ("ia", "ka"), None)),
        check_vma=False,
    )
```

profile of v0, /device:TPU:1, one launch (start us, length us, event | category | flops | bytes accessed | tf_op | source)
XLA Modules:
  0.0 827.5 jit_solution(4852424667202017735)
XLA Ops:
  8.0 1.4 convert_element_type.36
  9.5 2.0 fusion.34
  11.5 2.0 fusion.36
  13.5 0.7 compare_select_fusion.3
  14.2 0.8 select_reduce_fusion.4
  14.9 0.8 select_reduce_fusion.5
  16.4 1.1 convert_bitcast_fusion
  17.5 75.5 %all-gather.4.cloned.1.call-done = bf16[1,2048,256]{2,1,0:T(8,128)(2,1)} async-done(((bf16[1,32,256]{2,1,0:T(8,128)(2,1)}), bf16[1,2048,256]{2,1,0:T(8,128)(2,1)}) %all-gather.4.cloned.1.call-update) | async-done | bytes 1048592 | tf_op jit(solution)/shard_map/all_gather | solution.py:80
  93.0 1.8 gather_fusion
  94.8 23.3 %conditional.4 = (f32[2048,256]{1,0:T(8,128)}) conditional(s32[]{:T(128)} %bitcast.41, () %tuple.54, (s32[1,1,1,2]{3,2,1,0:T(1,128)}, bf16[512,256]{1,0:T(8,128)(2,1)S(1)}, bf16[1,1,1,2,128,128,128]{6,5,4,3,2,1,0:T(8,128)(2,1)}, s32[1,1,1,2]{3,2,1,0:T(1,128)}, bf16[2048,256]{1,0:T(8,128)(2,1)S(1)}, /*index=5*/s32[1,1,1,2]{3,2,1,0:T(1,128)}) %tuple.134), branch_computations={%region_6.0_spmd, %region_7.0_spmd} | conditional | flops 1082130432 | bytes 83099928 | solution.py:104
  95.5 2.8 slice.76
  98.3 2.4 convolution_bitcast_fusion
  100.7 6.7 copy.52
  107.6 8.2 multiply_reduce_fusion
  116.0 1.5 broadcast.140
  117.4 0.7 bitcast_dynamic-update-slice_fusion.2
  118.1 3.6 gather_fusion.1
  121.8 0.3 all-gather.6.cloned.1.call-start
  122.1 149.6 %all-reduce.7.cloned.1.call-done = (f32[256,256]{0,1:T(8,128)}, f32[256,256]{0,1:T(8,128)}) async-done(((f32[256,256]{0,1:T(8,128)}, f32[256,256]{0,1:T(8,128)}), (f32[256,256]{0,1:T(8,128)}, f32[256,256]{0,1:T(8,128)})) %all-reduce.7.cloned.1.call-update) | async-done | bytes 524304 | tf_op jit(solution)/shard_map/psum | solution.py:79
  271.6 1.1 mul.94
  272.9 11.7 %cholesky.130 = f32[128,128]{1,0:T(8,128)S(1)} custom-call(f32[128,128]{1,0:T(8,128)S(1)} %cholesky.194), custom_call_target="Cholesky" | custom-call | tf_op jit(solution)/shard_map/jit(cholesky)/cholesky | solution.py:10
  284.7 9.8 %custom-call.15 = f32[1,128,128]{1,2,0:T(8,128)S(1)} custom-call(f32[1,128,128]{2,1,0:T(8,128)S(1)} %get-tuple-element.155), custom_call_target="InvertDiagBlocksLowerTriangular" | custom-call | tf_op jit(solution)/shard_map/jit(cholesky)/cholesky | solution.py:10
  295.0 11.7 %cholesky.147 = f32[128,128]{1,0:T(8,128)S(1)} custom-call(f32[128,128]{1,0:T(8,128)S(1)} %convolution_subtract_fusion.1), custom_call_target="Cholesky" | custom-call | tf_op jit(solution)/shard_map/jit(cholesky)/cholesky | solution.py:10
  306.8 0.7 compare_reduce_fusion.2
  308.8 14.6 %while.4 = (s32[]{:T(128)}, f32[256,256]{1,0:T(8,128)S(1)}, s32[2,2]{1,0:T(2,128)S(1)}, f32[2,128,128]{2,1,0:T(8,128)S(1)}, s32[]{:T(128)}) while((s32[]{:T(128)}, f32[256,256]{1,0:T(8,128)S(1)}, s32[2,2]{1,0:T(2,128)S(1)}, f32[2,128,128]{2,1,0:T(8,128)S(1)}, s32[]{:T(128)}) %tuple.103), condition=%wide.while_cond, body=%wide.while_body.sunk | while | flops 2 | bytes 131181 | solution.py:11
  319.4 0.6 fusion.68
  320.0 1.4 bitcast_dynamic-update-slice_fusion.6
  321.4 0.6 fusion.68
  322.0 1.4 bitcast_dynamic-update-slice_fusion.6
  323.4 19.7 %custom-call.16 = f32[2,128,128]{1,2,0:T(8,128)S(1)} custom-call(f32[2,128,128]{2,1,0:T(8,128)S(1)} %get-tuple-element.124), custom_call_target="InvertDiagBlocksLowerTriangular" | custom-call | tf_op jit(solution)/shard_map/jit(_cho_solve)/triangular_solve | solution.py:11
  343.1 0.9 fusion.23
  344.0 0.9 convolution_subtract_fusion.5
  344.9 0.3 fusion.25
  345.9 77.9 %psum.37 = f32[256]{0:T(256)S(1)} all-reduce(f32[256]{0:T(256)S(1)} %multiply_reduce_fusion.5), channel_id=1, replica_groups=mesh['ia'=4,'ja'=4,'ka'=16] {'ia','ja','ka'}, use_global_device_ids=true, to_apply=%region_13.16 | all-reduce | flops 256 | bytes 2048 | tf_op jit(solution)/shard_map/psum | solution.py:111
  423.9 0.6 bitcast_convert_fusion.4
  424.6 1.1 fusion.46
  425.8 71.7 %all-gather.6.cloned.1.call-done = bf16[2048,256]{1,0:T(8,128)(2,1)} async-done(((bf16[32,256]{1,0:T(8,128)(2,1)}), bf16[2048,256]{1,0:T(8,128)(2,1)}) %all-gather.6.cloned.1.call-update) | async-done | bytes 1048592 | tf_op jit(solution)/shard_map/all_gather | solution.py:116
  497.5 1.8 gather_fusion.2
  499.4 23.6 %conditional.6 = (f32[2048,256]{1,0:T(8,128)}) conditional(s32[]{:T(128)} %bitcast.41, () %tuple.57, (s32[1,1,1,2]{3,2,1,0:T(1,128)S(1)}, bf16[2048,256]{1,0:T(8,128)(2,1)S(1)}, bf16[1,1,1,2,128,128,128]{6,5,4,3,2,1,0:T(8,128)(2,1)}, s32[1,1,1,2]{3,2,1,0:T(1,128)S(1)}, bf16[512,256]{1,0:T(8,128)(2,1)S(1)}, ...), branch_computations={%region_15.18_spmd, %region_16.19_spmd} | conditional | flops 1082130432 | bytes 83099800 | solution.py:139
  499.4 2.5 slice.84
  501.9 3.6 convolution_bitcast_fusion.2
  505.5 6.7 copy.55
  512.4 8.3 multiply_reduce_fusion.2
  520.8 1.5 broadcast.142
  522.3 0.7 bitcast_dynamic-update-slice_fusion.3
  523.1 3.7 gather_fusion.3
  526.8 150.8 %all-reduce.5.cloned.1.call-done = f32[256,256]{0,1:T(8,128)} async-done(((f32[256,256]{0,1:T(8,128)}), f32[256,256]{0,1:T(8,128)}) %all-reduce.5.cloned.1.call-update) | async-done | bytes 262160 | tf_op jit(solution)/shard_map/psum | solution.py:115
  677.6 1.0 mul.96
  678.8 11.7 %cholesky.164 = f32[128,128]{1,0:T(8,128)S(1)} custom-call(f32[128,128]{1,0:T(8,128)S(1)} %cholesky.197), custom_call_target="Cholesky" | custom-call | tf_op jit(solution)/shard_map/jit(cholesky)/cholesky | solution.py:10
  690.6 9.8 %custom-call.17 = f32[1,128,128]{1,2,0:T(8,128)S(1)} custom-call(f32[1,128,128]{2,1,0:T(8,128)S(1)} %get-tuple-element.151), custom_call_target="InvertDiagBlocksLowerTriangular" | custom-call | tf_op jit(solution)/shard_map/jit(cholesky)/cholesky | solution.py:10
  700.9 11.7 %cholesky.181 = f32[128,128]{1,0:T(8,128)S(1)} custom-call(f32[128,128]{1,0:T(8,128)S(1)} %convolution_subtract_fusion), custom_call_target="Cholesky" | custom-call | tf_op jit(solution)/shard_map/jit(cholesky)/cholesky | solution.py:10
  712.6 0.6 compare_reduce_fusion
  713.3 0.6 compare_reduce_fusion.1
  715.2 4.2 while.5
  715.5 0.6 fusion.69
  716.1 1.4 bitcast_dynamic-update-slice_fusion.7
  717.5 0.6 fusion.69
  718.1 1.4 bitcast_dynamic-update-slice_fusion.7
  719.4 19.7 %custom-call.18 = f32[2,128,128]{1,2,0:T(8,128)S(1)} custom-call(f32[2,128,128]{2,1,0:T(8,128)S(1)} %get-tuple-element.125), custom_call_target="InvertDiagBlocksLowerTriangular" | custom-call | tf_op jit(solution)/shard_map/jit(_cho_solve)/triangular_solve | solution.py:11
  739.2 0.9 fusion.27
  740.0 0.9 convolution_subtract_fusion.3
  741.0 0.3 fusion.29
  742.0 77.3 %psum.39 = f32[256]{0:T(256)S(1)} all-reduce(f32[256]{0:T(256)S(1)} %multiply_reduce_fusion.4), channel_id=1, replica_groups=mesh['ia'=4,'ja'=4,'ka'=16] {'ia','ja','ka'}, use_global_device_ids=true, to_apply=%region_22.25 | all-reduce | flops 256 | bytes 2048 | tf_op jit(solution)/shard_map/psum | solution.py:145
  819.3 0.6 divide_bitcast_fusion
  (77 shorter events, 4.0 us)
Async XLA Ops:
  8.0 85.0 %all-gather.4.cloned.1.call-start = ((), (), s32[]{:S(2)}) async-start(), calls=%async_computation.2 | async-start | bytes 1064960 | tf_op jit(solution)/shard_map/all_gather | solution.py:80
  9.4 262.2 %all-reduce.7.cloned.1.call-start = ((), (), s32[]{:S(2)}) async-start(), calls=%async_computation.7 | async-start | bytes 1048576 | tf_op jit(solution)/shard_map/psum | solution.py:79
  13.5 329.6 %reduce-scatter.3.cloned.1.call-start = ((), (), s32[]{:S(2)}) async-start(), calls=%async_computation.3 | async-start | bytes 2129920 | tf_op jit(solution)/shard_map/reduce_scatter | solution.py:109
  100.7 6.7 copy-start.4
  107.5 8.4 %copy-start.7 = (s32[1,1,1,2]{3,2,1,0:T(1,128)S(1)}, s32[1,1,1,2]{3,2,1,0:T(1,128)}, u32[]{:S(2)}) copy-start(s32[1,1,1,2]{3,2,1,0:T(1,128)} %get-tuple-element.85) | copy-start | bytes 28 | tf_op jit(solution)/shard_map/cond
  121.7 302.8 %copy-start.1 = (s32[64]{0:T(128)S(1)}, s32[64]{0:T(128)}, u32[]{:S(2)}) copy-start(s32[64]{0:T(128)} %param.25) | copy-start | bytes 772
  121.8 375.7 %all-gather.6.cloned.1.call-start = ((), (), s32[]{:S(2)}) async-start(), calls=%async_computation.6 | async-start | bytes 1064960 | tf_op jit(solution)/shard_map/all_gather | solution.py:116
  271.6 227.7 %copy-start.2 = (s32[1,1,1,2]{3,2,1,0:T(1,128)S(1)}, s32[1,1,1,2]{3,2,1,0:T(1,128)}, u32[]{:S(2)}) copy-start(s32[1,1,1,2]{3,2,1,0:T(1,128)} %param.23) | copy-start | bytes 28
  271.6 227.7 %copy-start.3 = (s32[1,1,1,2]{3,2,1,0:T(1,128)S(1)}, s32[1,1,1,2]{3,2,1,0:T(1,128)}, u32[]{:S(2)}) copy-start(s32[1,1,1,2]{3,2,1,0:T(1,128)} %param.22) | copy-start | bytes 28
  271.6 227.7 %copy-start.6 = (s32[1,1,1,2]{3,2,1,0:T(1,128)S(1)}, s32[1,1,1,2]{3,2,1,0:T(1,128)}, u32[]{:S(2)}) copy-start(s32[1,1,1,2]{3,2,1,0:T(1,128)} %param.21) | copy-start | bytes 28
  424.5 253.1 %all-reduce.5.cloned.1.call-start = ((), (), s32[]{:S(2)}) async-start(), calls=%async_computation.4 | async-start | bytes 524288 | tf_op jit(solution)/shard_map/psum | solution.py:115
  425.8 313.4 %reduce-scatter.5.cloned.1.call-start = ((), (), s32[]{:S(2)}) async-start(), calls=%async_computation.5 | async-start | bytes 2129920 | tf_op jit(solution)/shard_map/reduce_scatter | solution.py:143
  523.1 154.5 %copy-start = (f32[256,256]{0,1:T(8,128)S(1)}, f32[256,256]{0,1:T(8,128)}, u32[]{:S(2)}) copy-start(f32[256,256]{0,1:T(8,128)} %get-tuple-element.143) | copy-start | bytes 786436
Sparse Core Ops, SparseCore 0:
  12.2 80.7 all-gather.3
  121.9 159.1 reduce-scatter.2
  424.6 72.8 all-gather.5
  527.0 159.5 reduce-scatter.4
Sparse Core Ops, SparseCore 1:
  15.6 256.0 all-reduce.6
  431.3 246.2 all-reduce.4
where the time goes:
time: 837 us; the launch traced here: 827 us
  waiting for transfers between devices  448 us (54%)
  blocking collectives  155 us (19%)
  other arithmetic  133 us (16%)
  local copies, waits for them, and re-layouts  42.5 us (5%)
  between operations  19.3 us (2%)
  matrix products  17.4 us (2%)
  loops' own time  12.2 us (1%)
    psum x1, waiting for transfers between devices, body(): gram_a = lax.psum(local_a, ('ia', 'ja', 'ka'))  151 us
    psum x1, waiting for transfers between devices, body(): gram_b, gram_c = lax.psum((local_b, local_c), ('ia', 'ja', 'ka'))  150 us
    psum x1, blocking collectives, body(): squares_a = lax.psum(jnp.sum(a_hat * a_hat, axis=0), ('ia', 'ja', 'ka'))  77.9 us
    psum x1, blocking collectives, body(): squares_b = lax.psum(jnp.sum(b_hat * b_hat, axis=0), ('ia', 'ja', 'ka'))  77.3 us
    all_gather x1, waiting for transfers between devices, body(): lax.all_gather(factor_b.astype(jnp.bfloat16), ('ia', 'ka'), axis=1, tiled...  75.5 us
    all_gather x1, waiting for transfers between devices, body(): lax.all_gather(a_own.astype(jnp.bfloat16)[None], ('ja', 'ka'), axis=1, ti...  71.7 us
    another operation x13, other arithmetic, solve_rows(): lower = jnp.linalg.cholesky(gram)  68.6 us
    another operation x5, other arithmetic, solve_rows(): return jax.scipy.linalg.cho_solve((lower, True), rows.T).T  39.4 us
  transfers between devices with their start and end apart: 6, of which 4 were waited for; matrix products, arithmetic and copies ran while one was open for 22% of the time, Pallas kernels for 0%

commit v1 on v0

--- a/solution.py
+++ b/solution.py
@@ -142,7 +142,7 @@
     stored_two = to_stored(partial_two, owner_two, piece_rows)
     summed_two = lax.psum_scatter(stored_two, ("ia", "ka"), scatter_dimension=0, tiled=True)
     b_hat = solve_rows(gram_a * gram_c, summed_two)
-    squares_b = lax.psum(jnp.sum(b_hat * b_hat, axis=0), ("ia", "ja", "ka"))
+    squares_b = lax.psum(lax.psum(jnp.sum(b_hat * b_hat, axis=0), ("ja", "ka")), "ia")
     b_own = b_hat / jnp.sqrt(squares_b / total_one + EPS)
     return (a_own[None], b_own[None])
 

time: 837 us -> 896 us (1.070)
  blocking collectives: 155 us -> 211 us
    psum x1 -> x2, blocking collectives: 77.3 us -> 133 us  [the longest x1 126 us: body(): lax.psum(jnp.sum(b_hat * b_hat, axis=0), ('ja', 'ka'))]
  transfers between devices with their start and end apart: 6 -> 6, of which waited for: 4 -> 4; matrix products, arithmetic and copies ran while one was open for 22% -> 21% of each run, Pallas kernels for 0% -> 0%
where the time goes in v1:
time: 896 us; the launch traced here: 884 us
  waiting for transfers between devices  448 us (50%)
  blocking collectives  211 us (24%)
  other arithmetic  133 us (15%)
  local copies, waits for them, and re-layouts  42.5 us (5%)
  between operations  19.3 us (2%)
  matrix products  17.4 us (2%)
  loops' own time  12.2 us (1%)
    psum x1, waiting for transfers between devices, body(): gram_a = lax.psum(local_a, ('ia', 'ja', 'ka'))  151 us
    psum x1, waiting for transfers between devices, body(): gram_b, gram_c = lax.psum((local_b, local_c), ('ia', 'ja', 'ka'))  150 us
    psum x1, blocking collectives, body(): lax.psum(jnp.sum(b_hat * b_hat, axis=0), ('ja', 'ka'))  126 us
    psum x1, blocking collectives, body(): squares_a = lax.psum(jnp.sum(a_hat * a_hat, axis=0), ('ia', 'ja', 'ka'))  77.9 us
    all_gather x1, waiting for transfers between devices, body(): lax.all_gather(factor_b.astype(jnp.bfloat16), ('ia', 'ka'), axis=1, tiled...  75.5 us
    all_gather x1, waiting for transfers between devices, body(): lax.all_gather(a_own.astype(jnp.bfloat16)[None], ('ja', 'ka'), axis=1, ti...  71.7 us
    another operation x13, other arithmetic, solve_rows(): lower = jnp.linalg.cholesky(gram)  68.6 us
    another operation x5, other arithmetic, solve_rows(): return jax.scipy.linalg.cho_solve((lower, True), rows.T).T  39.4 us
  transfers between devices with their start and end apart: 6, of which 4 were waited for; matrix products, arithmetic and copies ran while one was open for 21% of the time, Pallas kernels for 0%

profile of v1, /device:TPU:1, one launch (start us, length us, event | category | flops | bytes accessed | tf_op | source)
XLA Modules:
  0.0 883.6 jit_solution(3957081961751890873)
XLA Ops:
  8.0 1.4 convert_element_type.36
  9.5 2.0 fusion.34
  11.5 2.0 fusion.36
  13.5 0.7 compare_select_fusion.3
  14.2 0.8 select_reduce_fusion.4
  14.9 0.8 select_reduce_fusion.5
  16.4 1.1 convert_bitcast_fusion
  17.5 75.5 %all-gather.4.cloned.1.call-done = bf16[1,2048,256]{2,1,0:T(8,128)(2,1)} async-done(((bf16[1,32,256]{2,1,0:T(8,128)(2,1)}), bf16[1,2048,256]{2,1,0:T(8,128)(2,1)}) %all-gather.4.cloned.1.call-update) | async-done | bytes 1048592 | tf_op jit(solution)/shard_map/all_gather | solution.py:80
  93.0 1.8 gather_fusion
  94.8 23.3 %conditional.4 = (f32[2048,256]{1,0:T(8,128)}) conditional(s32[]{:T(128)} %bitcast.41, () %tuple.54, (s32[1,1,1,2]{3,2,1,0:T(1,128)}, bf16[512,256]{1,0:T(8,128)(2,1)S(1)}, bf16[1,1,1,2,128,128,128]{6,5,4,3,2,1,0:T(8,128)(2,1)}, s32[1,1,1,2]{3,2,1,0:T(1,128)}, bf16[2048,256]{1,0:T(8,128)(2,1)S(1)}, /*index=5*/s32[1,1,1,2]{3,2,1,0:T(1,128)}) %tuple.134), branch_computations={%region_6.0_spmd, %region_7.0_spmd} | conditional | flops 1082130432 | bytes 83099928 | solution.py:104
  95.5 2.8 slice.76
  98.3 2.4 convolution_bitcast_fusion
  100.7 6.7 copy.52
  107.6 8.2 multiply_reduce_fusion
  116.0 1.5 broadcast.140
  117.4 0.7 bitcast_dynamic-update-slice_fusion.2
  118.1 3.6 gather_fusion.1
  121.8 0.3 all-gather.6.cloned.1.call-start
  122.1 149.6 %all-reduce.7.cloned.1.call-done = (f32[256,256]{0,1:T(8,128)}, f32[256,256]{0,1:T(8,128)}) async-done(((f32[256,256]{0,1:T(8,128)}, f32[256,256]{0,1:T(8,128)}), (f32[256,256]{0,1:T(8,128)}, f32[256,256]{0,1:T(8,128)})) %all-reduce.7.cloned.1.call-update) | async-done | bytes 524304 | tf_op jit(solution)/shard_map/psum | solution.py:79
  271.6 1.1 mul.94
  272.9 11.7 %cholesky.130 = f32[128,128]{1,0:T(8,128)S(1)} custom-call(f32[128,128]{1,0:T(8,128)S(1)} %cholesky.194), custom_call_target="Cholesky" | custom-call | tf_op jit(solution)/shard_map/jit(cholesky)/cholesky | solution.py:10
  284.7 9.8 %custom-call.15 = f32[1,128,128]{1,2,0:T(8,128)S(1)} custom-call(f32[1,128,128]{2,1,0:T(8,128)S(1)} %get-tuple-element.155), custom_call_target="InvertDiagBlocksLowerTriangular" | custom-call | tf_op jit(solution)/shard_map/jit(cholesky)/cholesky | solution.py:10
  295.0 11.7 %cholesky.147 = f32[128,128]{1,0:T(8,128)S(1)} custom-call(f32[128,128]{1,0:T(8,128)S(1)} %convolution_subtract_fusion.1), custom_call_target="Cholesky" | custom-call | tf_op jit(solution)/shard_map/jit(cholesky)/cholesky | solution.py:10
  306.8 0.7 compare_reduce_fusion.2
  308.8 14.6 %while.4 = (s32[]{:T(128)}, f32[256,256]{1,0:T(8,128)S(1)}, s32[2,2]{1,0:T(2,128)S(1)}, f32[2,128,128]{2,1,0:T(8,128)S(1)}, s32[]{:T(128)}) while((s32[]{:T(128)}, f32[256,256]{1,0:T(8,128)S(1)}, s32[2,2]{1,0:T(2,128)S(1)}, f32[2,128,128]{2,1,0:T(8,128)S(1)}, s32[]{:T(128)}) %tuple.103), condition=%wide.while_cond, body=%wide.while_body.sunk | while | flops 2 | bytes 131181 | solution.py:11
  319.4 0.6 fusion.68
  320.0 1.4 bitcast_dynamic-update-slice_fusion.6
  321.4 0.6 fusion.68
  322.0 1.4 bitcast_dynamic-update-slice_fusion.6
  323.4 19.7 %custom-call.16 = f32[2,128,128]{1,2,0:T(8,128)S(1)} custom-call(f32[2,128,128]{2,1,0:T(8,128)S(1)} %get-tuple-element.124), custom_call_target="InvertDiagBlocksLowerTriangular" | custom-call | tf_op jit(solution)/shard_map/jit(_cho_solve)/triangular_solve | solution.py:11
  343.1 0.9 fusion.23
  344.0 0.9 convolution_subtract_fusion.5
  345.9 77.9 %psum.44 = f32[256]{0:T(256)S(1)} all-reduce(f32[256]{0:T(256)S(1)} %multiply_reduce_fusion.5), channel_id=1, replica_groups=mesh['ia'=4,'ja'=4,'ka'=16] {'ia','ja','ka'}, use_global_device_ids=true, to_apply=%region_13.16 | all-reduce | flops 256 | bytes 2048 | tf_op jit(solution)/shard_map/psum | solution.py:111
  423.9 0.6 bitcast_convert_fusion.4
  424.6 1.1 fusion.46
  425.8 71.7 %all-gather.6.cloned.1.call-done = bf16[2048,256]{1,0:T(8,128)(2,1)} async-done(((bf16[32,256]{1,0:T(8,128)(2,1)}), bf16[2048,256]{1,0:T(8,128)(2,1)}) %all-gather.6.cloned.1.call-update) | async-done | bytes 1048592 | tf_op jit(solution)/shard_map/all_gather | solution.py:116
  497.5 1.8 gather_fusion.2
  499.4 23.6 %conditional.6 = (f32[2048,256]{1,0:T(8,128)}) conditional(s32[]{:T(128)} %bitcast.41, () %tuple.57, (s32[1,1,1,2]{3,2,1,0:T(1,128)S(1)}, bf16[2048,256]{1,0:T(8,128)(2,1)S(1)}, bf16[1,1,1,2,128,128,128]{6,5,4,3,2,1,0:T(8,128)(2,1)}, s32[1,1,1,2]{3,2,1,0:T(1,128)S(1)}, bf16[512,256]{1,0:T(8,128)(2,1)S(1)}, ...), branch_computations={%region_15.18_spmd, %region_16.19_spmd} | conditional | flops 1082130432 | bytes 83099800 | solution.py:139
  499.4 2.5 slice.84
  501.9 3.6 convolution_bitcast_fusion.2
  505.5 6.7 copy.55
  512.4 8.3 multiply_reduce_fusion.2
  520.8 1.5 broadcast.142
  522.3 0.7 bitcast_dynamic-update-slice_fusion.3
  523.1 3.7 gather_fusion.3
  526.8 150.8 %all-reduce.5.cloned.1.call-done = f32[256,256]{0,1:T(8,128)} async-done(((f32[256,256]{0,1:T(8,128)}), f32[256,256]{0,1:T(8,128)}) %all-reduce.5.cloned.1.call-update) | async-done | bytes 262160 | tf_op jit(solution)/shard_map/psum | solution.py:115
  677.6 1.0 mul.96
  678.8 11.7 %cholesky.164 = f32[128,128]{1,0:T(8,128)S(1)} custom-call(f32[128,128]{1,0:T(8,128)S(1)} %cholesky.197), custom_call_target="Cholesky" | custom-call | tf_op jit(solution)/shard_map/jit(cholesky)/cholesky | solution.py:10
  690.6 9.8 %custom-call.17 = f32[1,128,128]{1,2,0:T(8,128)S(1)} custom-call(f32[1,128,128]{2,1,0:T(8,128)S(1)} %get-tuple-element.151), custom_call_target="InvertDiagBlocksLowerTriangular" | custom-call | tf_op jit(solution)/shard_map/jit(cholesky)/cholesky | solution.py:10
  700.9 11.7 %cholesky.181 = f32[128,128]{1,0:T(8,128)S(1)} custom-call(f32[128,128]{1,0:T(8,128)S(1)} %convolution_subtract_fusion), custom_call_target="Cholesky" | custom-call | tf_op jit(solution)/shard_map/jit(cholesky)/cholesky | solution.py:10
  712.6 0.6 compare_reduce_fusion
  713.3 0.6 compare_reduce_fusion.1
  715.2 4.2 while.5
  715.5 0.6 fusion.69
  716.1 1.4 bitcast_dynamic-update-slice_fusion.7
  717.5 0.6 fusion.69
  718.1 1.4 bitcast_dynamic-update-slice_fusion.7
  719.4 19.7 %custom-call.18 = f32[2,128,128]{1,2,0:T(8,128)S(1)} custom-call(f32[2,128,128]{2,1,0:T(8,128)S(1)} %get-tuple-element.125), custom_call_target="InvertDiagBlocksLowerTriangular" | custom-call | tf_op jit(solution)/shard_map/jit(_cho_solve)/triangular_solve | solution.py:11
  739.2 0.9 fusion.27
  740.0 0.9 convolution_subtract_fusion.3
  741.0 0.3 fusion.29
  742.0 125.6 %psum.46 = f32[256]{0:T(256)S(1)} all-reduce(f32[256]{0:T(256)S(1)} %multiply_reduce_fusion.4), channel_id=1, replica_groups=mesh['ia'=4,'ja'=4,'ka'=16] {'ja','ka'}, use_global_device_ids=true, to_apply=%region_22.25 | all-reduce | flops 256 | bytes 2048 | tf_op jit(solution)/shard_map/psum | solution.py:145
  867.5 7.9 psum.47
  875.4 0.6 divide_bitcast_fusion
  (78 shorter events, 4.3 us)
Async XLA Ops:
  8.0 85.0 %all-gather.4.cloned.1.call-start = ((), (), s32[]{:S(2)}) async-start(), calls=%async_computation.2 | async-start | bytes 1064960 | tf_op jit(solution)/shard_map/all_gather | solution.py:80
  9.4 262.2 %all-reduce.7.cloned.1.call-start = ((), (), s32[]{:S(2)}) async-start(), calls=%async_computation.7 | async-start | bytes 1048576 | tf_op jit(solution)/shard_map/psum | solution.py:79
  13.5 329.6 %reduce-scatter.3.cloned.1.call-start = ((), (), s32[]{:S(2)}) async-start(), calls=%async_computation.3 | async-start | bytes 2129920 | tf_op jit(solution)/shard_map/reduce_scatter | solution.py:109
  100.7 6.7 copy-start.4
  107.5 8.4 copy-start.7
  121.7 302.8 %copy-start.1 = (s32[64]{0:T(128)S(1)}, s32[64]{0:T(128)}, u32[]{:S(2)}) copy-start(s32[64]{0:T(128)} %param.25) | copy-start | bytes 772
  121.8 375.7 %all-gather.6.cloned.1.call-start = ((), (), s32[]{:S(2)}) async-start(), calls=%async_computation.6 | async-start | bytes 1064960 | tf_op jit(solution)/shard_map/all_gather | solution.py:116
  271.6 227.7 %copy-start.2 = (s32[1,1,1,2]{3,2,1,0:T(1,128)S(1)}, s32[1,1,1,2]{3,2,1,0:T(1,128)}, u32[]{:S(2)}) copy-start(s32[1,1,1,2]{3,2,1,0:T(1,128)} %param.23) | copy-start | bytes 28
  271.6 227.7 %copy-start.3 = (s32[1,1,1,2]{3,2,1,0:T(1,128)S(1)}, s32[1,1,1,2]{3,2,1,0:T(1,128)}, u32[]{:S(2)}) copy-start(s32[1,1,1,2]{3,2,1,0:T(1,128)} %param.22) | copy-start | bytes 28
  271.6 227.7 %copy-start.6 = (s32[1,1,1,2]{3,2,1,0:T(1,128)S(1)}, s32[1,1,1,2]{3,2,1,0:T(1,128)}, u32[]{:S(2)}) copy-start(s32[1,1,1,2]{3,2,1,0:T(1,128)} %param.21) | copy-start | bytes 28
  424.5 253.1 %all-reduce.5.cloned.1.call-start = ((), (), s32[]{:S(2)}) async-start(), calls=%async_computation.4 | async-start | bytes 524288 | tf_op jit(solution)/shard_map/psum | solution.py:115
  425.8 313.4 %reduce-scatter.5.cloned.1.call-start = ((), (), s32[]{:S(2)}) async-start(), calls=%async_computation.5 | async-start | bytes 2129920 | tf_op jit(solution)/shard_map/reduce_scatter | solution.py:143
  523.1 154.5 %copy-start = (f32[256,256]{0,1:T(8,128)S(1)}, f32[256,256]{0,1:T(8,128)}, u32[]{:S(2)}) copy-start(f32[256,256]{0,1:T(8,128)} %get-tuple-element.143) | copy-start | bytes 786436
Sparse Core Ops, SparseCore 0:
  12.2 80.7 all-gather.3
  121.9 159.1 reduce-scatter.2
  424.6 72.8 all-gather.5
  527.0 159.5 reduce-scatter.4
Sparse Core Ops, SparseCore 1:
  15.6 256.0 all-reduce.6
  431.3 246.2 all-reduce.4
